TPU v7x, 256 devices: a whole 4x4x8 slice. The times are simulated.
256 devices in a mesh: seq: 32 (over y_hi, z, core), mp: 8 (over y_lo, x).
Axes of the slice: x: 4, y: 4 (y_hi: 2, y_lo: 2; y = y_hi * 2 + y_lo), z: 8, core: 2. Of those that a mesh axis runs over, the one named last changes fastest.
Arguments:
- tokens: bfloat16 [8192, 4096], P('seq', 'mp'), may hold values from -16 to 16
- grad_out: bfloat16 [8192, 4096], P('seq', 'mp'), may hold values from -6 to 6
- w_query: bfloat16 [4096, 4096], P('seq', 'mp'), may hold values from -0.09375 to 0.09375
- w_key: bfloat16 [4096, 1024], P('seq', 'mp'), may hold values from -0.09375 to 0.09375
- w_value: bfloat16 [4096, 1024], P('seq', 'mp'), may hold values from -0.09375 to 0.09375
- doc_lengths: int32 [4], replicated, may hold values from 1 to 48, 64 in all
Outputs:
- grad_tokens: bfloat16 [8192, 4096], P('seq', 'mp')
- grad_w_query: float32 [4096, 4096], P('seq', 'mp')
- grad_w_key: float32 [4096, 1024], P('seq', 'mp')
- grad_w_value: float32 [4096, 1024], P('seq', 'mp')
Inputs may be any that keep to these rules, and one draw needn't show every extreme that they name: `doc_lengths`: the lengths sum to 64.
All inputs are finite; a program needn't handle non-finite values.
Results may differ from a plain program's by a relative error of at most 0.03.
The roundings to bfloat16 on the way count: a program that leaves them out, or rounds other values in their place, can miss the bound.
Values may be sent and summed in bfloat16 or wider, within the bound.
No kernel may reach another device: no remote copies, remote signals or barrier semaphores. Data moves between devices by JAX's collectives and lax.ppermute only.
A program may use at most 64 MiB of HBM per device.

v0:
```python
import jax
import jax.numpy as jnp
from jax import lax
from jax.sharding import PartitionSpec as P

HEAD_DIM = 128
WINDOW = 4096
ALIGN = 128
THETA = 10000.0
CONTRACT_LAST = (((1,), (1,)), ((), ()))
CONTRACT_FIRST = (((0,), (0,)), ((), ()))


def from_everyone(value, axis):
    peers = lax.axis_size(axis)
    return lax.all_to_all(
        jnp.broadcast_to(value[None], (peers, *value.shape)), axis, 0, 0, tiled=True
    )


def in_order(parts, dim):
    parts = jnp.moveaxis(parts, 0, dim)
    dims = parts.shape
    return parts.reshape(*dims[:dim], dims[dim] * dims[dim + 1], *dims[dim + 2 :])


def gather_directly(value, axis, dim):
    parts = from_everyone(value, axis)
    return in_order(parts, dim)


def shifted(value, axis, by):
    peers = lax.axis_size(axis)
    pairs = [(i, i + by) for i in range(peers) if 0 <= i + by < peers]
    return lax.ppermute(value, axis, pairs)


def split_up(value, dim, peers):
    dims = value.shape
    parts = value.reshape(*dims[:dim], peers, dims[dim] // peers, *dims[dim + 1 :])
    return jnp.moveaxis(parts, dim, 0)


def summed_on_arrival(value, axis, dim):
    peers = lax.axis_size(axis)
    parts = lax.all_to_all(split_up(value, dim, peers), axis, 0, 0, tiled=True)
    return jnp.sum(parts.astype(jnp.float32), axis=0)


def list_offsets(positions, ends, lengths):
    after = positions[:, None] >= ends[None, :]
    member = jnp.sum(after.astype(jnp.int32), axis=1)
    before = jnp.sum(jnp.where(after, lengths[None, :] * ALIGN, 0), axis=1)
    return (member, positions - before)


def rope_tables(offsets):
    half = HEAD_DIM // 2
    inverse = THETA ** (-(jnp.arange(half, dtype=jnp.float32) * 2.0 / HEAD_DIM))
    angle = offsets.astype(jnp.float32)[:, None] * inverse[None, :]
    angle = jnp.concatenate([angle, angle], axis=1)
    return (jnp.cos(angle), jnp.sin(angle))


def rotate(vectors, cosine, sine, direction):
    half = vectors.shape[-1] // 2
    turned = jnp.concatenate([-vectors[..., half:], vectors[..., :half]], axis=-1)
    return vectors * cosine[:, None, :] + direction * turned * sine[:, None, :]


def local(tokens, grad_out, w_query, w_key, w_value, doc_lengths):
    rows = tokens.shape[0]
    head_cols = w_query.shape[1]
    kv_cols = w_key.shape[1]
    heads_here = head_cols // HEAD_DIM
    kv_here = kv_cols // HEAD_DIM
    group = heads_here // kv_here
    span = WINDOW // rows
    block = min(512, WINDOW)
    count = WINDOW // block
    scale = HEAD_DIM ** (-0.5)
    first = lax.axis_index("seq") * rows
    ends = jnp.cumsum(doc_lengths) * ALIGN
    own_pos = first + jnp.arange(rows, dtype=jnp.int32)
    own_member, own_offset = list_offsets(own_pos, ends, doc_lengths)
    cosine, sine = rope_tables(own_offset)
    weights_all = jnp.concatenate([w_query, w_key, w_value], axis=1)
    whole = gather_directly(tokens, "mp", 1)
    panel = lax.all_gather(weights_all, "seq", axis=0, tiled=True)
    projected = jnp.dot(whole, panel, preferred_element_type=jnp.float32)
    query = rotate(projected[:, :head_cols].reshape(rows, heads_here, HEAD_DIM), cosine, sine, 1.0)
    query = query.astype(jnp.bfloat16).reshape(rows, kv_here, group, HEAD_DIM)
    keys = rotate(
        projected[:, head_cols : head_cols + kv_cols].reshape(rows, kv_here, HEAD_DIM),
        cosine,
        sine,
        1.0,
    ).astype(jnp.bfloat16)
    values = projected[:, head_cols + kv_cols :].astype(jnp.bfloat16)
    keys_flat = keys.reshape(rows, kv_cols)
    levels = (span - 1).bit_length()
    hops = [1] + [2**level for level in range(levels)]
    stack = (keys_flat[None], values[None])
    for number, hop in enumerate(hops):
        arrived = shifted((stack[0], stack[1]), "seq", hop)
        if number == 0:
            stack = arrived
        else:
            stack = (
                jnp.concatenate([arrived[0], stack[0]], axis=0),
                jnp.concatenate([arrived[1], stack[1]], axis=0),
            )
    window_keys, window_values = (stack[0], stack[1])
    window_keys = window_keys.reshape(count, block, kv_here, HEAD_DIM)
    window_values = window_values.reshape(count, block, kv_here, HEAD_DIM)
    window_pos = first - WINDOW + jnp.arange(WINDOW, dtype=jnp.int32)
    window_member, _ = list_offsets(window_pos, ends, doc_lengths)
    window_pos = window_pos.reshape(count, block)
    window_member = window_member.reshape(count, block)
    own_values = values.reshape(rows, kv_here, HEAD_DIM)

    def scores_for(key_block, key_pos, key_member):
        raw = (
            jnp.einsum("qagd,kad->agqk", query, key_block, preferred_element_type=jnp.float32)
            * scale
        )
        gap = own_pos[:, None] - key_pos[None, :]
        live = (
            (key_pos[None, :] >= 0)
            & (gap >= 0)
            & (gap < WINDOW)
            & (own_member[:, None] == key_member[None, :])
        )
        return jnp.where(live, raw, -jnp.inf)

    first_scores = scores_for(keys, own_pos, own_member)
    top = jnp.max(first_scores, axis=-1)
    mass = jnp.sum(jnp.exp(first_scores - top[..., None]), axis=-1)

    def absorb(carry, inputs):
        top, mass = carry
        key_block, key_pos, key_member = inputs
        scores = scores_for(key_block, key_pos, key_member)
        new_top = jnp.maximum(top, jnp.max(scores, axis=-1))
        factor = jnp.exp(top - new_top)
        mass = mass * factor + jnp.sum(jnp.exp(scores - new_top[..., None]), axis=-1)
        return ((new_top, mass), None)

    (top, mass), _ = lax.scan(absorb, (top, mass), (window_keys, window_pos, window_member))
    log_total = top + jnp.log(mass)

    def attend_part(key_block, value_block, key_pos, key_member):
        scores = scores_for(key_block, key_pos, key_member)
        probs_low = jnp.exp(scores - log_total[..., None]).astype(jnp.bfloat16)
        return jnp.einsum(
            "agqk,kad->agqd", probs_low, value_block, preferred_element_type=jnp.float32
        )

    def attend_step(total, inputs):
        return (total + attend_part(*inputs), None)

    attended = attend_part(keys, own_values, own_pos, own_member)
    attended, _ = lax.scan(
        attend_step, attended, (window_keys, window_values, window_pos, window_member)
    )
    grad_heads = grad_out.reshape(rows, kv_here, group, HEAD_DIM)
    delta = jnp.einsum("qagd,agqd->agq", grad_heads.astype(jnp.float32), attended)

    def differentiate(key_block, value_block, key_pos, key_member):
        scores = scores_for(key_block, key_pos, key_member)
        probs = jnp.exp(scores - log_total[..., None])
        probs_low = probs.astype(jnp.bfloat16)
        grad_values = jnp.einsum(
            "agqk,qagd->kad", probs_low, grad_heads, preferred_element_type=jnp.float32
        )
        grad_probs = jnp.einsum(
            "qagd,kad->agqk", grad_heads, value_block, preferred_element_type=jnp.float32
        )
        grad_scores = (probs * (grad_probs - delta[..., None])).astype(jnp.bfloat16)
        grad_query = (
            jnp.einsum("agqk,kad->qagd", grad_scores, key_block, preferred_element_type=jnp.float32)
            * scale
        )
        grad_keys = (
            jnp.einsum("agqk,qagd->kad", grad_scores, query, preferred_element_type=jnp.float32)
            * scale
        )
        return (grad_query, grad_keys, grad_values)

    query_grad, own_key_grad, own_value_grad = differentiate(keys, own_values, own_pos, own_member)

    def visit(total, inputs):
        grad_query, grad_keys, grad_values = differentiate(*inputs)
        return (total + grad_query, (grad_keys, grad_values))

    query_grad, (far_keys, far_values) = lax.scan(
        visit, query_grad, (window_keys, window_values, window_pos, window_member)
    )
    far_keys = far_keys.reshape(span, rows, kv_cols)
    far_values = far_values.reshape(span, rows, kv_cols)
    levels = (span - 1).bit_length()
    extra = 2**levels - span
    filler = jnp.zeros((extra, rows, kv_cols), jnp.float32)
    stack = (
        jnp.concatenate([far_keys[::-1], filler], axis=0),
        jnp.concatenate([far_values[::-1], filler], axis=0),
    )
    hops = [2**level for level in reversed(range(levels))] + [1]
    for number, hop in enumerate(hops):
        if number < levels:
            moving = (stack[0][hop:], stack[1][hop:])
        else:
            moving = stack
        arrived = (
            shifted(moving[0].astype(jnp.bfloat16), "seq", -hop).astype(jnp.float32),
            shifted(moving[1].astype(jnp.bfloat16), "seq", -hop).astype(jnp.float32),
        )
        if number < levels:
            stack = (stack[0][:hop] + arrived[0], stack[1][:hop] + arrived[1])
        else:
            stack = arrived
    returned = (stack[0][0], stack[1][0])
    key_grad = own_key_grad.reshape(rows, kv_cols) + returned[0]
    value_grad = own_value_grad.reshape(rows, kv_cols) + returned[1]
    grad_query = (
        rotate(query_grad.reshape(rows, heads_here, HEAD_DIM), cosine, sine, -1.0)
        .astype(jnp.bfloat16)
        .reshape(rows, head_cols)
    )
    grad_key = (
        rotate(key_grad.reshape(rows, kv_here, HEAD_DIM), cosine, sine, -1.0)
        .astype(jnp.bfloat16)
        .reshape(rows, kv_cols)
    )
    grad_value = value_grad.astype(jnp.bfloat16)
    grad_all = jnp.concatenate([grad_query, grad_key, grad_value], axis=1)
    term = lax.dot_general(grad_all, panel, CONTRACT_LAST, preferred_element_type=jnp.float32)
    grad_tokens = summed_on_arrival(term.astype(jnp.bfloat16), "mp", 1).astype(jnp.bfloat16)
    grad_weights = lax.psum_scatter(
        lax.dot_general(whole, grad_all, CONTRACT_FIRST, preferred_element_type=jnp.float32).astype(
            jnp.bfloat16
        ),
        "seq",
        scatter_dimension=0,
        tiled=True,
    ).astype(jnp.float32)
    return (
        grad_tokens,
        grad_weights[:, :head_cols],
        grad_weights[:, head_cols : head_cols + kv_cols],
        grad_weights[:, head_cols + kv_cols :],
    )


def solution(mesh):
    placed = (P("seq", "mp"), P("seq", "mp"), P("seq", "mp"), P("seq", "mp"), P("seq", "mp"), P())
    return jax.shard_map(
        local,
        mesh=mesh,
        in_specs=placed,
        out_specs=(P("seq", "mp"), P("seq", "mp"), P("seq", "mp"), P("seq", "mp")),
        check_vma=False,
    )
```

profile of v0, /device:TPU:2, one launch (start us, length us, event | category | flops | bytes accessed | tf_op | source)
XLA Modules:
  0.0 652.3 jit_solution(11152818374100308907)
XLA Ops:
  7.2 1.6 pad_maximum_fusion.5
  10.0 1.5 broadcast_in_dim.60
  11.5 6.0 all-to-all-start
  22.0 21.4 %all-to-all-done = bf16[8,256,512]{1,2,0:T(8,128)(2,1)S(1)} async-done(((bf16[8,256,512]{1,2,0:T(8,128)(2,1)}), bf16[8,256,512]{1,2,0:T(8,128)(2,1)S(1)}, u32[]{:S(2)}, u32[]{:S(2)}) %all-to-all-start) | async-done | bytes 2097184 | tf_op jit(solution)/shard_map/all_to_all | solution.py:16
  43.3 76.7 %all-gather.2.cloned.1.call-done = bf16[4096,768]{1,0:T(8,128)(2,1)} async-done(((bf16[128,768]{1,0:T(8,128)(2,1)}), bf16[4096,768]{1,0:T(8,128)(2,1)}) %all-gather.2.cloned.1.call-update) | async-done | bytes 6291472 | tf_op jit(solution)/shard_map/all_gather | solution.py:89
  120.1 4.6 convolution_bitcast_fusion.4
  125.9 2.1 collective-permute-start
  128.1 3.7 collective-permute-start.5
  132.1 1.5 collective-permute-start.1
  135.8 3.7 collective-permute-start.6
  140.2 3.5 collective-permute-start.2
  146.2 2.6 collective-permute-start.7
  149.8 3.6 collective-permute-start.3
  154.5 1.6 pad_maximum_fusion.4
  156.1 4.2 collective-permute-start.8
  160.4 5.0 collective-permute-done.3
  166.1 1.8 pad_maximum_fusion
  167.9 7.8 %collective-permute-start.4 = (bf16[8,256,128]{1,2,0:T(8,128)(2,1)}, bf16[8,256,128]{1,2,0:T(8,128)(2,1)}, u32[]{:S(2)}, u32[]{:S(2)}) collective-permute-start(bf16[8,256,128]{1,2,0:T(8,128)(2,1)} %pad_maximum_fusion), channel_id=1, source_target_pairs={{0,64},{8,72},{16,80},{24,88},{32,96},{40,104},{48,112},{56,120},{... | collective-permute-start | bytes 1572872 | tf_op jit(solution)/shard_map/ppermute | solution.py:35
  177.6 1.7 fusion.85
  179.3 1.9 pad_maximum_fusion.1
  181.3 17.1 %collective-permute-start.9 = (bf16[8,256,128]{1,2,0:T(8,128)(2,1)}, bf16[8,256,128]{1,2,0:T(8,128)(2,1)}, u32[]{:S(2)}, u32[]{:S(2)}) collective-permute-start(bf16[8,256,128]{1,2,0:T(8,128)(2,1)} %pad_maximum_fusion.1), channel_id=1, source_target_pairs={{0,64},{8,72},{16,80},{24,88},{32,96},{40,104},{48,112},{56,120},{... | collective-permute-start | bytes 1572872 | tf_op jit(solution)/shard_map/ppermute | solution.py:35
  198.4 1.9 constant_dynamic-update-slice_fusion.4
  201.0 1.6 constant_dynamic-update-slice_fusion.2
  203.8 2.3 copy.140
  206.1 14.3 %collective-permute-done.9 = bf16[8,256,128]{1,2,0:T(8,128)(2,1)} collective-permute-done((bf16[8,256,128]{1,2,0:T(8,128)(2,1)}, bf16[8,256,128]{1,2,0:T(8,128)(2,1)}, u32[]{:S(2)}, u32[]{:S(2)}) %collective-permute-start.9) | collective-permute-done | bytes 524320 | tf_op jit(solution)/shard_map/ppermute | solution.py:35
  220.4 1.9 constant_dynamic-update-slice_fusion.9
  222.2 1.7 constant_dynamic-update-slice_fusion.8
  227.5 2.3 copy.149
  229.8 29.3 %while.39 = (s32[]{:T(128)}, f32[1,4,256]{2,1,0:T(4,128)S(1)}, f32[1,4,256]{2,1,0:T(4,128)S(1)}, s32[8,512]{1,0:T(8,128)}, s32[256]{0:T(256)S(1)}, /*index=5*/s3...) while((s32[]{:T(128)}, f32[1,4,256]{2,1,0:T(4,128)S(1)}, ...), condition=%wide.region_9.10_spmd.clone, body=%wide.region_6.9_spmd.clone.sunk | while | flops 138808064 | bytes 5050493 | solution.py:149
  260.3 37.7 %while.40 = (s32[]{:T(128)}, f32[1,4,256,128]{3,2,1,0:T(8,128)}, s32[8,512]{1,0:T(8,128)}, s32[256]{0:T(256)S(1)}, s32[8,512]{1,0:T(8,128)}, /*index=5*/bf16[8,5...) while((s32[]{:T(128)}, f32[1,4,256,128]{3,2,1,0:T(8,128)}, ...), condition=%wide.region_11.12_spmd.clone, body=%wide.region_10.11_spmd.clone.sunk | while | flops 271581952 | bytes 1856641 | solution.py:163
  262.1 3.0 fusion.161
  266.8 3.0 fusion.161
  271.5 3.0 fusion.161
  276.2 3.0 fusion.161
  280.9 3.0 fusion.161
  285.6 3.0 fusion.161
  290.4 3.0 fusion.161
  295.1 3.0 fusion.161
  298.0 1.5 multiply_reduce_fusion
  302.8 65.6 %while.41 = (s32[]{:T(128)}, f32[256,1,4,128]{0,3,2,1:T(8,128)S(1)}, f32[8,512,1,128]{3,1,2,0:T(8,128)}, f32[8,512,1,128]{3,1,2,0:T(8,128)}, bf16[8,512,1,128]{3...) while((s32[]{:T(128)}, ...), condition=%wide.region_13.14_spmd.clone, body=%wide.region_12.13_spmd.clone.sunk | while | flops 676004608 | bytes 12738741 | solution.py:196
  304.6 1.5 fusion.173
  312.8 1.5 fusion.173
  321.0 1.5 fusion.173
  329.2 1.5 fusion.173
  345.6 1.5 fusion.173
  368.4 2.1 slice.169
  373.9 2.1 slice.179
  376.1 2.1 copy.169
  378.2 1.9 slice.231
  382.8 2.3 slice.168
  386.2 2.6 copy.161
  388.8 2.6 copy.167
  391.4 2.3 collective-permute-done.10
  396.7 2.6 collective-permute-done.15
  402.3 18.1 %collective-permute-done.11 = bf16[4,256,128]{1,2,0:T(8,128)(2,1)S(1)} collective-permute-done((bf16[4,256,128]{1,2,0:T(8,128)(2,1)S(1)}, bf16[4,256,128]{1,2,0:T(8,128)(2,1)S(1)}, u32[]{:S(2)}, u32[]{:S(2)}) %collective-permute-start.11) | collective-permute-done | bytes 262176 | tf_op jit(solution)/shard_map/ppermute | solution.py:35
  421.9 12.4 %collective-permute-done.16 = bf16[4,256,128]{1,2,0:T(8,128)(2,1)S(1)} collective-permute-done((bf16[4,256,128]{1,2,0:T(8,128)(2,1)S(1)}, bf16[4,256,128]{1,2,0:T(8,128)(2,1)S(1)}, u32[]{:S(2)}, u32[]{:S(2)}) %collective-permute-start.16) | collective-permute-done | bytes 262176 | tf_op jit(solution)/shard_map/ppermute | solution.py:35
  435.8 25.6 %collective-permute-done.12 = bf16[2,256,128]{1,2,0:T(8,128)(2,1)S(1)} collective-permute-done((bf16[2,256,128]{1,2,0:T(8,128)(2,1)S(1)}, bf16[2,256,128]{1,2,0:T(8,128)(2,1)S(1)}, u32[]{:S(2)}, u32[]{:S(2)}) %collective-permute-start.12) | collective-permute-done | bytes 131104 | tf_op jit(solution)/shard_map/ppermute | solution.py:35
  462.8 6.2 collective-permute-done.17
  474.7 3.0 collective-permute-done.19
  477.7 4.4 fusion.68
  482.2 8.6 %copy.196 = bf16[4096,768]{1,0:T(8,128)(2,1)} copy(bf16[4096,768]{0,1:T(8,128)(2,1)} %fusion.68) | data formatting | bytes 12582912
  490.8 4.6 convolution_convert_fusion.1
  495.7 30.4 %all_to_all.10 = bf16[8,256,512]{2,1,0:T(8,128)(2,1)S(1)} all-to-all(bf16[8,256,512]{2,1,0:T(8,128)(2,1)S(1)} %bitcast.388), channel_id=1, replica_groups=mesh['seq'=32,'mp'=8] {'mp'}, dimensions={0} | all-to-all | bytes 4194304 | tf_op jit(solution)/shard_map/all_to_all | solution.py:46
  527.1 114.9 %reduce-scatter.4.cloned.1.call-done = bf16[128,768]{1,0:T(8,128)(2,1)} async-done(((bf16[4096,768]{1,0:T(8,128)(2,1)}), bf16[128,768]{1,0:T(8,128)(2,1)}) %reduce-scatter.4.cloned.1.call-update) | async-done | bytes 196624
  (334 shorter events, 155.2 us)
Async XLA Ops:
  7.2 112.9 %all-gather.2.cloned.1.call-start = ((), (), s32[]{:S(2)}) async-start(), calls=%async_computation.3 | async-start | bytes 6488064 | tf_op jit(solution)/shard_map/all_gather | solution.py:89
  11.5 6.0 copy-start.11
  11.5 6.2 copy-start.26
  11.5 31.8 %all-to-all-start = ((bf16[8,256,512]{1,2,0:T(8,128)(2,1)}), bf16[8,256,512]{1,2,0:T(8,128)(2,1)S(1)}, u32[]{:S(2)}, u32[]{:S(2)}) async-start(bf16[8,256,512]{1,2,0:T(8,128)(2,1)} %broadcast_in_dim.60), calls=%async_computation | async-start | bytes 4194304 | tf_op jit(solution)/shard_map/all_to_all | solution.py:16
  17.5 624.5 %reduce-scatter.4.cloned.1.call-start = ((), (), s32[]{:S(2)}) async-start(), calls=%async_computation.4 | async-start | bytes 6488064
  43.3 81.4 %copy-start = (bf16[8,256,512]{1,2,0:T(8,128)(2,1)}, bf16[8,256,512]{1,2,0:T(8,128)(2,1)S(1)}, u32[]{:S(2)}) copy-start(bf16[8,256,512]{1,2,0:T(8,128)(2,1)S(1)} %all-to-all-done) | copy-start | bytes 6291460
  120.1 4.7 copy-start.24
  125.9 6.2 copy-start.20
  125.9 6.2 collective-permute-start
  128.1 7.7 %collective-permute-start.5 = (bf16[1,256,128]{1,2,0:T(8,128)(2,1)S(1)}, bf16[1,256,128]{1,2,0:T(8,128)(2,1)}, u32[]{:S(2)}, u32[]{:S(2)}) collective-permute-start(bf16[1,256,128]{1,2,0:T(8,128)(2,1)S(1)} %fusion.117), channel_id=1, source_target_pairs={{0,8},{8,16},{16,24},{24,32},{32,40},{40,48},{48,56},{56,64},{64,7... | collective-permute-start | bytes 196616 | tf_op jit(solution)/shard_map/ppermute | solution.py:35
  132.1 11.6 %copy-start.14 = (bf16[1,256,128]{1,2,0:T(8,128)(2,1)}, bf16[1,256,128]{1,2,0:T(8,128)(2,1)S(1)}, u32[]{:S(2)}) copy-start(bf16[1,256,128]{1,2,0:T(8,128)(2,1)S(1)} %collective-permute-done) | copy-start | bytes 196612
  132.1 7.5 %collective-permute-start.1 = (bf16[1,256,128]{1,2,0:T(8,128)(2,1)S(1)}, bf16[1,256,128]{1,2,0:T(8,128)(2,1)S(1)}, u32[]{:S(2)}, u32[]{:S(2)}) collective-permute-start(bf16[1,256,128]{1,2,0:T(8,128)(2,1)S(1)} %collective-permute-done), channel_id=1, source_target_pairs={{0,8},{8,16},{16,24},{24,32},{32,40},{40,48},{48,56},{56,64},{64,7... | collective-permute-start | bytes 196616 | tf_op jit(solution)/shard_map/ppermute | solution.py:35
  135.8 9.5 %collective-permute-start.6 = (bf16[1,256,128]{1,2,0:T(8,128)(2,1)}, bf16[1,256,128]{1,2,0:T(8,128)(2,1)}, u32[]{:S(2)}, u32[]{:S(2)}) collective-permute-start(bf16[1,256,128]{1,2,0:T(8,128)(2,1)} %collective-permute-done.5), channel_id=1, source_target_pairs={{0,8},{8,16},{16,24},{24,32},{32,40},{40,48},{48,56},{56,64},{64,7... | collective-permute-start | bytes 196616 | tf_op jit(solution)/shard_map/ppermute | solution.py:35
  139.5 4.1 copy-start.17
  140.2 8.6 %collective-permute-start.2 = (bf16[2,256,128]{1,2,0:T(8,128)(2,1)}, bf16[2,256,128]{1,2,0:T(8,128)(2,1)}, u32[]{:S(2)}, u32[]{:S(2)}) collective-permute-start(bf16[2,256,128]{1,2,0:T(8,128)(2,1)} %pad_maximum_fusion.9), channel_id=1, source_target_pairs={{0,16},{8,24},{16,32},{24,40},{32,48},{40,56},{48,64},{56,72},{64,... | collective-permute-start | bytes 393224 | tf_op jit(solution)/shard_map/ppermute | solution.py:35
  145.0 8.5 %copy-start.2 = (f32[256,4,128]{2,0,1:T(8,128)}, f32[256,4,128]{2,0,1:T(8,128)S(1)}, u32[]{:S(2)}) copy-start(f32[256,4,128]{2,0,1:T(8,128)S(1)} %maximum_multiply_fusion) | copy-start | bytes 1572868
  145.2 8.3 %copy-start.21 = (bf16[256,128]{0,1:T(8,128)(2,1)S(1)}, bf16[256,128]{0,1:T(8,128)(2,1)}, u32[]{:S(2)}) copy-start(bf16[256,128]{0,1:T(8,128)(2,1)} %copy-done.20) | copy-start | bytes 196612
  145.2 8.3 %copy-start.23 = (pred[256,256]{0,1:T(8,128)(4,1)S(1)}, pred[256,256]{0,1:T(8,128)(4,1)}, u32[]{:S(2)}) copy-start(pred[256,256]{0,1:T(8,128)(4,1)} %fusion.89) | copy-start | bytes 196612
  145.2 20.9 %copy-start.15 = (bf16[1,256,128]{1,2,0:T(8,128)(2,1)S(1)}, bf16[1,256,128]{1,2,0:T(8,128)(2,1)}, u32[]{:S(2)}) copy-start(bf16[1,256,128]{1,2,0:T(8,128)(2,1)} %copy-done.14) | copy-start | bytes 196612
  145.2 20.9 %copy-start.18 = (bf16[1,256,128]{1,2,0:T(8,128)(2,1)S(1)}, bf16[1,256,128]{1,2,0:T(8,128)(2,1)}, u32[]{:S(2)}) copy-start(bf16[1,256,128]{1,2,0:T(8,128)(2,1)} %copy-done.17) | copy-start | bytes 196612
  146.2 7.6 %collective-permute-start.7 = (bf16[2,256,128]{1,2,0:T(8,128)(2,1)S(1)}, bf16[2,256,128]{1,2,0:T(8,128)(2,1)S(1)}, u32[]{:S(2)}, u32[]{:S(2)}) collective-permute-start(bf16[2,256,128]{1,2,0:T(8,128)(2,1)S(1)} %pad_maximum_fusion.10), channel_id=1, source_target_pairs={{0,16},{8,24},{16,32},{24,40},{32,48},{40,56},{48,64},{56,72},{64,... | collective-permute-start | bytes 393224 | tf_op jit(solution)/shard_map/ppermute | solution.py:35
  149.8 15.6 %collective-permute-start.3 = (bf16[4,256,128]{1,2,0:T(8,128)(2,1)S(1)}, bf16[4,256,128]{1,2,0:T(8,128)(2,1)S(1)}, u32[]{:S(2)}, u32[]{:S(2)}) collective-permute-start(bf16[4,256,128]{1,2,0:T(8,128)(2,1)S(1)} %pad_maximum_fusion.3), channel_id=1, source_target_pairs={{0,32},{8,40},{16,48},{24,56},{32,64},{40,72},{48,80},{56,88},{64,... | collective-permute-start | bytes 786440 | tf_op jit(solution)/shard_map/ppermute | solution.py:35
  153.8 0.7 copy-start.9
  156.1 23.2 %collective-permute-start.8 = (bf16[4,256,128]{1,2,0:T(8,128)(2,1)}, bf16[4,256,128]{1,2,0:T(8,128)(2,1)}, u32[]{:S(2)}, u32[]{:S(2)}) collective-permute-start(bf16[4,256,128]{1,2,0:T(8,128)(2,1)} %pad_maximum_fusion.4), channel_id=1, source_target_pairs={{0,32},{8,40},{16,48},{24,56},{32,64},{40,72},{48,80},{56,88},{64,... | collective-permute-start | bytes 786440 | tf_op jit(solution)/shard_map/ppermute | solution.py:35
  165.4 0.7 copy-start.12
  167.9 30.5 %collective-permute-start.4 = (bf16[8,256,128]{1,2,0:T(8,128)(2,1)}, bf16[8,256,128]{1,2,0:T(8,128)(2,1)}, u32[]{:S(2)}, u32[]{:S(2)}) collective-permute-start(bf16[8,256,128]{1,2,0:T(8,128)(2,1)} %pad_maximum_fusion), channel_id=1, source_target_pairs={{0,64},{8,72},{16,80},{24,88},{32,96},{40,104},{48,112},{56,120},{... | collective-permute-start | bytes 1572872 | tf_op jit(solution)/shard_map/ppermute | solution.py:35
  177.6 1.7 copy-start.10
  177.6 22.6 %copy-start.13 = (bf16[4,256,128]{1,2,0:T(8,128)(2,1)S(1)}, bf16[4,256,128]{1,2,0:T(8,128)(2,1)}, u32[]{:S(2)}) copy-start(bf16[4,256,128]{1,2,0:T(8,128)(2,1)} %copy-done.12) | copy-start | bytes 786436
  177.6 24.9 %copy-start.19 = (bf16[1,256,128]{1,2,0:T(8,128)(2,1)S(1)}, bf16[1,256,128]{1,2,0:T(8,128)(2,1)}, u32[]{:S(2)}) copy-start(bf16[1,256,128]{1,2,0:T(8,128)(2,1)} %copy-done.17) | copy-start | bytes 196612
  177.6 25.5 %copy-start.16 = (bf16[1,256,128]{1,2,0:T(8,128)(2,1)S(1)}, bf16[1,256,128]{1,2,0:T(8,128)(2,1)}, u32[]{:S(2)}) copy-start(bf16[1,256,128]{1,2,0:T(8,128)(2,1)} %copy-done.14) | copy-start | bytes 196612
  181.3 39.1 %collective-permute-start.9 = (bf16[8,256,128]{1,2,0:T(8,128)(2,1)}, bf16[8,256,128]{1,2,0:T(8,128)(2,1)}, u32[]{:S(2)}, u32[]{:S(2)}) collective-permute-start(bf16[8,256,128]{1,2,0:T(8,128)(2,1)} %pad_maximum_fusion.1), channel_id=1, source_target_pairs={{0,64},{8,72},{16,80},{24,88},{32,96},{40,104},{48,112},{56,120},{... | collective-permute-start | bytes 1572872 | tf_op jit(solution)/shard_map/ppermute | solution.py:35
  300.9 0.8 copy-start.4
  372.6 21.2 %collective-permute-start.10 = (bf16[8,256,128]{1,2,0:T(8,128)(2,1)}, bf16[8,256,128]{1,2,0:T(8,128)(2,1)}, u32[]{:S(2)}, u32[]{:S(2)}) collective-permute-start(bf16[8,256,128]{1,2,0:T(8,128)(2,1)} %slice.232), channel_id=1, source_target_pairs={{64,0},{72,8},{80,16},{88,24},{96,32},{104,40},{112,48},{120,56},{... | collective-permute-start | bytes 1572872 | tf_op jit(solution)/shard_map/ppermute | solution.py:35
  373.8 7.6 %copy-start.3 = (f32[256,4,128]{2,0,1:T(8,128)S(1)}, f32[256,4,128]{2,0,1:T(8,128)}, u32[]{:S(2)}) copy-start(f32[256,4,128]{2,0,1:T(8,128)} %copy-done.2) | copy-start | bytes 1572868
  373.9 7.6 %copy-start.7 = (f32[256,128]{1,0:T(8,128)S(1)}, f32[256,128]{1,0:T(8,128)}, u32[]{:S(2)}) copy-start(f32[256,128]{1,0:T(8,128)} %copy.132) | copy-start | bytes 393220
  380.0 5.1 copy-start.8
  380.0 19.3 %collective-permute-start.15 = (bf16[8,256,128]{1,2,0:T(8,128)(2,1)}, bf16[8,256,128]{1,2,0:T(8,128)(2,1)}, u32[]{:S(2)}, u32[]{:S(2)}) collective-permute-start(bf16[8,256,128]{1,2,0:T(8,128)(2,1)} %slice.231), channel_id=1, source_target_pairs={{64,0},{72,8},{80,16},{88,24},{96,32},{104,40},{112,48},{120,56},{... | collective-permute-start | bytes 1572872 | tf_op jit(solution)/shard_map/ppermute | solution.py:35
  386.2 5.2 copy-start.22
  391.4 8.0 %copy-start.5 = (f32[8,256,128]{1,2,0:T(8,128)S(1)}, f32[8,256,128]{1,2,0:T(8,128)}, u32[]{:S(2)}) copy-start(f32[8,256,128]{1,2,0:T(8,128)} %copy.167) | copy-start | bytes 3145732
  395.3 6.6 %copy-start.6 = (bf16[256,4,128]{0,2,1:T(8,128)(2,1)S(1)}, bf16[256,4,128]{0,2,1:T(8,128)(2,1)}, u32[]{:S(2)}) copy-start(bf16[256,4,128]{0,2,1:T(8,128)(2,1)} %copy.165) | copy-start | bytes 786436
  395.3 25.1 %collective-permute-start.11 = (bf16[4,256,128]{1,2,0:T(8,128)(2,1)S(1)}, bf16[4,256,128]{1,2,0:T(8,128)(2,1)S(1)}, u32[]{:S(2)}, u32[]{:S(2)}) collective-permute-start(bf16[4,256,128]{1,2,0:T(8,128)(2,1)S(1)} %slice.234), channel_id=1, source_target_pairs={{32,0},{40,8},{48,16},{56,24},{64,32},{72,40},{80,48},{88,56},{96,... | collective-permute-start | bytes 786440 | tf_op jit(solution)/shard_map/ppermute | solution.py:35
  400.6 33.8 %collective-permute-start.16 = (bf16[4,256,128]{1,2,0:T(8,128)(2,1)S(1)}, bf16[4,256,128]{1,2,0:T(8,128)(2,1)S(1)}, u32[]{:S(2)}, u32[]{:S(2)}) collective-permute-start(bf16[4,256,128]{1,2,0:T(8,128)(2,1)S(1)} %slice.233), channel_id=1, source_target_pairs={{32,0},{40,8},{48,16},{56,24},{64,32},{72,40},{80,48},{88,56},{96,... | collective-permute-start | bytes 786440 | tf_op jit(solution)/shard_map/ppermute | solution.py:35
  420.5 53.8 %copy-start.25 = (f32[256,1,64]{0,2,1:T(8,128)S(1)}, f32[256,1,64]{0,2,1:T(8,128)}, u32[]{:S(2)}) copy-start(f32[256,1,64]{0,2,1:T(8,128)} %get-tuple-element.466) | copy-start | bytes 196612
  420.5 41.0 %collective-permute-start.12 = (bf16[2,256,128]{1,2,0:T(8,128)(2,1)S(1)}, bf16[2,256,128]{1,2,0:T(8,128)(2,1)S(1)}, u32[]{:S(2)}, u32[]{:S(2)}) collective-permute-start(bf16[2,256,128]{1,2,0:T(8,128)(2,1)S(1)} %slice.236), channel_id=1, source_target_pairs={{16,0},{24,8},{32,16},{40,24},{48,32},{56,40},{64,48},{72,56},{80,... | collective-permute-start | bytes 393224 | tf_op jit(solution)/shard_map/ppermute | solution.py:35
  434.4 43.4 %copy-start.1 = (bf16[8,256,512]{1,2,0:T(8,128)(2,1)S(1)}, bf16[8,256,512]{1,2,0:T(8,128)(2,1)}, u32[]{:S(2)}) copy-start(bf16[8,256,512]{1,2,0:T(8,128)(2,1)} %copy-done) | copy-start | bytes 6291460
  434.4 34.6 %collective-permute-start.17 = (bf16[2,256,128]{1,2,0:T(8,128)(2,1)S(1)}, bf16[2,256,128]{1,2,0:T(8,128)(2,1)S(1)}, u32[]{:S(2)}, u32[]{:S(2)}) collective-permute-start(bf16[2,256,128]{1,2,0:T(8,128)(2,1)S(1)} %slice.235), channel_id=1, source_target_pairs={{16,0},{24,8},{32,16},{40,24},{48,32},{56,40},{64,48},{72,56},{80,... | collective-permute-start | bytes 393224 | tf_op jit(solution)/shard_map/ppermute | solution.py:35
  461.5 8.9 %collective-permute-start.13 = (bf16[1,256,128]{1,2,0:T(8,128)(2,1)S(1)}, bf16[1,256,128]{1,2,0:T(8,128)(2,1)S(1)}, u32[]{:S(2)}, u32[]{:S(2)}) collective-permute-start(bf16[1,256,128]{1,2,0:T(8,128)(2,1)S(1)} %slice.238), channel_id=1, source_target_pairs={{8,0},{16,8},{24,16},{32,24},{40,32},{48,40},{56,48},{64,56},{72,6... | collective-permute-start | bytes 196616 | tf_op jit(solution)/shard_map/ppermute | solution.py:35
  469.1 3.1 collective-permute-start.18
  470.4 3.8 collective-permute-start.14
  472.2 5.5 collective-permute-start.19
Sparse Core Ops, SparseCore 0:
  11.3 108.6 all-gather.1
  491.0 151.0 reduce-scatter.3
where the time goes:
time: 658 us; the launch traced here: 652 us
  waiting for transfers between devices  304 us (46%)
  matrix products  105 us (16%)
  local copies, waits for them, and re-layouts  75.4 us (11%)
  starting transfers between devices  69.7 us (11%)
  other arithmetic  52.3 us (8%)
  blocking collectives  30.4 us (5%)
  between operations  14.8 us (2%)
    unnamed x3, waiting for transfers between devices  115 us
    ppermute x20, waiting for transfers between devices, shifted(): return lax.ppermute(value, axis, pairs)  90.6 us
    all_gather x1, waiting for transfers between devices, local(): panel = lax.all_gather(weights_all, 'seq', axis=0, tiled=True)  76.7 us
    ppermute x20, starting transfers between devices, shifted(): return lax.ppermute(value, axis, pairs)  63.7 us
    all_to_all x1, blocking collectives, summed_on_arrival(): parts = lax.all_to_all(split_up(value, dim, peers), axis, 0, 0, tiled=True)  30.4 us
    unnamed x70, local copies, waits for them, and re-layouts  26.1 us
    dot_general x9, matrix products, attend_part(): jnp.einsum('agqk,kad->agqd', probs_low, value_block, preferred_element_ty...  24.9 us
    dot_general x17, matrix products, scores_for(): jnp.einsum('qagd,kad->agqk', query, key_block, preferred_element_type=jnp...  23.5 us
  transfers between devices with their start and end apart: 23, of which 14 were waited for; matrix products, arithmetic and copies ran while one was open for 9% of the time, Pallas kernels for 0%

commit v1 on v0

--- a/solution.py
+++ b/solution.py
@@ -86,7 +86,9 @@
     cosine, sine = rope_tables(own_offset)
     weights_all = jnp.concatenate([w_query, w_key, w_value], axis=1)
     whole = gather_directly(tokens, "mp", 1)
-    panel = lax.all_gather(weights_all, "seq", axis=0, tiled=True)
+    panel = jnp.concatenate(
+        lax.all_to_all(jnp.stack([weights_all] * lax.axis_size("seq")), "seq", 0, 0), axis=0
+    )
     projected = jnp.dot(whole, panel, preferred_element_type=jnp.float32)
     query = rotate(projected[:, :head_cols].reshape(rows, heads_here, HEAD_DIM), cosine, sine, 1.0)
     query = query.astype(jnp.bfloat16).reshape(rows, kv_here, group, HEAD_DIM)

time: 658 us -> 717 us (1.090)
  waiting for transfers between devices: 304 us -> 344 us
  starting transfers between devices: 69.7 us -> 82.6 us
    all_to_all x0 -> x1, waiting for transfers between devices: none -> 138 us  [local(): lax.all_to_all(jnp.stack([weights_all] * lax.axis_size('seq')), 'seq', 0, 0)]
    all_gather x1 -> x0, waiting for transfers between devices: 76.7 us -> none  [local(): panel = lax.all_gather(weights_all, 'seq', axis=0, tiled=True)]
    ppermute x20, waiting for transfers between devices: 90.6 us -> 69.2 us  [shifted(): return lax.ppermute(value, axis, pairs)]
    all_to_all x0 -> x1, starting transfers between devices: none -> 11.4 us  [local(): lax.all_to_all(jnp.stack([weights_all] * lax.axis_size('seq')), 'seq', 0, 0)]
    unnamed x3 -> x2, waiting for transfers between devices: 115 us -> 111 us
    unnamed x70 -> x76, local copies, waits for them, and re-layouts: 26.1 us -> 26.2 us
  transfers between devices with their start and end apart: 23 -> 23, of which waited for: 14 -> 14; matrix products, arithmetic and copies ran while one was open for 9% -> 8% of each run, Pallas kernels for 0% -> 0%
where the time goes in v1:
time: 717 us; the launch traced here: 712 us
  waiting for transfers between devices  344 us (48%)
  matrix products  106 us (15%)
  starting transfers between devices  82.6 us (12%)
  local copies, waits for them, and re-layouts  78.8 us (11%)
  other arithmetic  50.7 us (7%)
  blocking collectives  34.2 us (5%)
  between operations  14.9 us (2%)
    all_to_all x1, waiting for transfers between devices, local(): lax.all_to_all(jnp.stack([weights_all] * lax.axis_size('seq')), 'seq', 0, 0)  138 us
    unnamed x2, waiting for transfers between devices  111 us
    ppermute x20, waiting for transfers between devices, shifted(): return lax.ppermute(value, axis, pairs)  69.2 us
    ppermute x20, starting transfers between devices, shifted(): return lax.ppermute(value, axis, pairs)  65.2 us
    all_to_all x1, blocking collectives, summed_on_arrival(): parts = lax.all_to_all(split_up(value, dim, peers), axis, 0, 0, tiled=True)  34.2 us
    unnamed x76, local copies, waits for them, and re-layouts  26.2 us
    all_to_all x1, waiting for transfers between devices, from_everyone(): lax.all_to_all(jnp.broadcast_to(value[None], (peers, *value.shape)), axis...  25.7 us
    dot_general x9, matrix products, attend_part(): jnp.einsum('agqk,kad->agqd', probs_low, value_block, preferred_element_ty...  25.5 us
  transfers between devices with their start and end apart: 23, of which 14 were waited for; matrix products, arithmetic and copies ran while one was open for 8% of the time, Pallas kernels for 0%

profile of v1, /device:TPU:2, one launch (start us, length us, event | category | flops | bytes accessed | tf_op | source)
XLA Modules:
  0.0 711.8 jit_solution(14812257508585160456)
XLA Ops:
  9.7 6.0 all-to-all-start.1
  15.8 25.7 %all-to-all-done.1 = bf16[8,256,512]{1,2,0:T(8,128)(2,1)S(1)} async-done(((bf16[8,256,512]{1,2,0:T(8,128)(2,1)}), bf16[8,256,512]{1,2,0:T(8,128)(2,1)S(1)}, u32[]{:S(2)}, u32[]{:S(2)}) %all-to-all-start.1) | async-done | bytes 2097184 | tf_op jit(solution)/shard_map/all_to_all | solution.py:16
  41.5 3.3 stack.2
  44.8 11.4 %all-to-all-start = ((bf16[32,128,768]{2,1,0:T(8,128)(2,1)}), bf16[32,128,768]{2,1,0:T(8,128)(2,1)}, u32[]{:S(2)}, u32[]{:S(2)}) async-start(bf16[32,128,768]{2,1,0:T(8,128)(2,1)} %stack.2), calls=%async_computation | async-start | bytes 12582912 | tf_op jit(solution)/shard_map/all_to_all | solution.py:90
  60.8 137.8 %all-to-all-done = bf16[32,128,768]{2,1,0:T(8,128)(2,1)} async-done(((bf16[32,128,768]{2,1,0:T(8,128)(2,1)}), bf16[32,128,768]{2,1,0:T(8,128)(2,1)}, u32[]{:S(2)}, u32[]{:S(2)}) %all-to-all-start) | async-done | bytes 6291488 | tf_op jit(solution)/shard_map/all_to_all | solution.py:90
  198.7 4.6 convolution_bitcast_fusion.4
  205.8 2.3 collective-permute-start.5
  211.9 4.0 collective-permute-start.6
  216.5 6.5 collective-permute-start.2
  225.5 2.6 collective-permute-start.7
  229.2 2.7 collective-permute-start.3
  232.9 1.6 pad_maximum_fusion.4
  234.5 4.1 collective-permute-start.8
  238.6 4.3 collective-permute-done.3
  243.7 1.8 pad_maximum_fusion
  245.4 15.7 %collective-permute-start.4 = (bf16[8,256,128]{1,2,0:T(8,128)(2,1)}, bf16[8,256,128]{1,2,0:T(8,128)(2,1)}, u32[]{:S(2)}, u32[]{:S(2)}) collective-permute-start(bf16[8,256,128]{1,2,0:T(8,128)(2,1)} %pad_maximum_fusion), channel_id=1, source_target_pairs={{0,64},{8,72},{16,80},{24,88},{32,96},{40,104},{48,112},{56,120},{... | collective-permute-start | bytes 1572872 | tf_op jit(solution)/shard_map/ppermute | solution.py:35
  263.1 1.7 fusion.85
  264.8 2.0 pad_maximum_fusion.1
  266.7 11.0 %collective-permute-start.9 = (bf16[8,256,128]{1,2,0:T(8,128)(2,1)}, bf16[8,256,128]{1,2,0:T(8,128)(2,1)}, u32[]{:S(2)}, u32[]{:S(2)}) collective-permute-start(bf16[8,256,128]{1,2,0:T(8,128)(2,1)} %pad_maximum_fusion.1), channel_id=1, source_target_pairs={{0,64},{8,72},{16,80},{24,88},{32,96},{40,104},{48,112},{56,120},{... | collective-permute-start | bytes 1572872 | tf_op jit(solution)/shard_map/ppermute | solution.py:35
  278.3 1.9 constant_dynamic-update-slice_fusion.4
  280.9 1.6 constant_dynamic-update-slice_fusion.2
  283.7 2.3 copy.140
  286.0 13.4 %collective-permute-done.9 = bf16[8,256,128]{1,2,0:T(8,128)(2,1)} collective-permute-done((bf16[8,256,128]{1,2,0:T(8,128)(2,1)}, bf16[8,256,128]{1,2,0:T(8,128)(2,1)}, u32[]{:S(2)}, u32[]{:S(2)}) %collective-permute-start.9) | collective-permute-done | bytes 524320 | tf_op jit(solution)/shard_map/ppermute | solution.py:35
  299.4 1.9 constant_dynamic-update-slice_fusion.9
  301.3 1.7 constant_dynamic-update-slice_fusion.8
  306.5 2.3 copy.149
  308.9 29.3 %while.39 = (s32[]{:T(128)}, f32[1,4,256]{2,1,0:T(4,128)S(1)}, f32[1,4,256]{2,1,0:T(4,128)S(1)}, s32[8,512]{1,0:T(8,128)}, s32[256]{0:T(256)S(1)}, /*index=5*/s3...) while((s32[]{:T(128)}, f32[1,4,256]{2,1,0:T(4,128)S(1)}, ...), condition=%wide.region_9.10_spmd.clone, body=%wide.region_6.9_spmd.clone.sunk | while | flops 138808064 | bytes 5050493 | solution.py:151
  339.5 38.3 %while.40 = (s32[]{:T(128)}, f32[1,4,256,128]{3,2,1,0:T(8,128)}, s32[8,512]{1,0:T(8,128)}, s32[256]{0:T(256)S(1)}, s32[8,512]{1,0:T(8,128)}, /*index=5*/bf16[8,5...) while((s32[]{:T(128)}, f32[1,4,256,128]{3,2,1,0:T(8,128)}, ...), condition=%wide.region_11.12_spmd.clone, body=%wide.region_10.11_spmd.clone.sunk | while | flops 271581952 | bytes 1856641 | solution.py:165
  341.2 3.0 fusion.161
  346.0 3.0 fusion.161
  350.8 3.0 fusion.161
  355.6 3.0 fusion.161
  360.4 3.0 fusion.161
  365.1 3.0 fusion.161
  369.9 3.0 fusion.161
  374.7 3.0 fusion.161
  377.7 1.5 multiply_reduce_fusion
  382.6 65.6 %while.41 = (s32[]{:T(128)}, f32[256,1,4,128]{0,3,2,1:T(8,128)S(1)}, f32[8,512,1,128]{3,1,2,0:T(8,128)}, f32[8,512,1,128]{3,1,2,0:T(8,128)}, bf16[8,512,1,128]{3...) while((s32[]{:T(128)}, ...), condition=%wide.region_13.14_spmd.clone, body=%wide.region_12.13_spmd.clone.sunk | while | flops 676004608 | bytes 12738741 | solution.py:198
  392.6 1.5 fusion.173
  400.7 1.5 fusion.173
  408.9 1.5 fusion.173
  417.1 1.5 fusion.173
  425.3 1.5 fusion.173
  433.5 1.5 fusion.173
  441.7 1.5 fusion.173
  448.2 2.1 slice.169
  453.7 2.1 slice.179
  455.9 2.0 copy.169
  457.9 1.9 slice.231
  462.6 2.3 slice.168
  465.9 2.7 copy.161
  468.6 2.5 copy.167
  471.2 4.7 collective-permute-done.10
  478.9 3.7 collective-permute-done.15
  485.5 26.4 %collective-permute-done.11 = bf16[4,256,128]{1,2,0:T(8,128)(2,1)S(1)} collective-permute-done((bf16[4,256,128]{1,2,0:T(8,128)(2,1)S(1)}, bf16[4,256,128]{1,2,0:T(8,128)(2,1)S(1)}, u32[]{:S(2)}, u32[]{:S(2)}) %collective-permute-start.11) | collective-permute-done | bytes 262176 | tf_op jit(solution)/shard_map/ppermute | solution.py:35
  513.4 8.9 %collective-permute-done.16 = bf16[4,256,128]{1,2,0:T(8,128)(2,1)S(1)} collective-permute-done((bf16[4,256,128]{1,2,0:T(8,128)(2,1)S(1)}, bf16[4,256,128]{1,2,0:T(8,128)(2,1)S(1)}, u32[]{:S(2)}, u32[]{:S(2)}) %collective-permute-start.16) | collective-permute-done | bytes 262176 | tf_op jit(solution)/shard_map/ppermute | solution.py:35
  525.2 4.2 collective-permute-done.17
  532.6 1.5 collective-permute-start.19
  535.1 2.1 collective-permute-done.19
  537.2 4.4 fusion.68
  541.6 8.6 %copy.196 = bf16[4096,768]{1,0:T(8,128)(2,1)} copy(bf16[4096,768]{0,1:T(8,128)(2,1)} %fusion.68) | data formatting | bytes 12582912
  550.3 4.6 convolution_convert_fusion.1
  555.1 34.2 %all_to_all.15 = bf16[8,256,512]{2,1,0:T(8,128)(2,1)S(1)} all-to-all(bf16[8,256,512]{2,1,0:T(8,128)(2,1)S(1)} %bitcast.389), channel_id=1, replica_groups=mesh['seq'=32,'mp'=8] {'mp'}, dimensions={0} | all-to-all | bytes 4194304 | tf_op jit(solution)/shard_map/all_to_all | solution.py:46
  590.4 111.1 %reduce-scatter.4.cloned.1.call-done = bf16[128,768]{1,0:T(8,128)(2,1)} async-done(((bf16[4096,768]{1,0:T(8,128)(2,1)}), bf16[128,768]{1,0:T(8,128)(2,1)}) %reduce-scatter.4.cloned.1.call-update) | async-done | bytes 196624
  (340 shorter events, 155.4 us)
Async XLA Ops:
  9.7 6.0 copy-start.26
  9.7 6.0 copy-start.27
  9.7 6.0 copy-start.28
  9.7 31.7 %all-to-all-start.1 = ((bf16[8,256,512]{1,2,0:T(8,128)(2,1)}), bf16[8,256,512]{1,2,0:T(8,128)(2,1)S(1)}, u32[]{:S(2)}, u32[]{:S(2)}) async-start(bf16[8,256,512]{1,2,0:T(8,128)(2,1)} %broadcast_in_dim.60), calls=%async_computation.1 | async-start | bytes 4194304 | tf_op jit(solution)/shard_map/all_to_all | solution.py:16
  41.5 157.2 %copy-start = (bf16[8,256,512]{1,2,0:T(8,128)(2,1)}, bf16[8,256,512]{1,2,0:T(8,128)(2,1)S(1)}, u32[]{:S(2)}) copy-start(bf16[8,256,512]{1,2,0:T(8,128)(2,1)S(1)} %all-to-all-done.1) | copy-start | bytes 6291460
  44.8 11.5 %copy-start.11 = (bf16[256,512]{1,0:T(8,128)(2,1)S(1)}, bf16[256,512]{1,0:T(8,128)(2,1)}, u32[]{:S(2)}) copy-start(bf16[256,512]{1,0:T(8,128)(2,1)} %param.13) | copy-start | bytes 786436
  44.8 11.7 %copy-start.29 = (s32[4]{0:T(128)S(1)}, s32[4]{0:T(128)}, u32[]{:S(2)}) copy-start(s32[4]{0:T(128)} %param.17) | copy-start | bytes 52
  44.8 153.8 %all-to-all-start = ((bf16[32,128,768]{2,1,0:T(8,128)(2,1)}), bf16[32,128,768]{2,1,0:T(8,128)(2,1)}, u32[]{:S(2)}, u32[]{:S(2)}) async-start(bf16[32,128,768]{2,1,0:T(8,128)(2,1)} %stack.2), calls=%async_computation | async-start | bytes 12582912 | tf_op jit(solution)/shard_map/all_to_all | solution.py:90
  56.3 645.2 %reduce-scatter.4.cloned.1.call-start = ((), (), s32[]{:S(2)}) async-start(), calls=%async_computation.4 | async-start | bytes 6488064
  198.7 4.7 copy-start.24
  204.5 3.9 copy-start.20
  204.5 3.9 collective-permute-start
  205.8 6.0 collective-permute-start.5
  208.4 14.6 %copy-start.14 = (bf16[1,256,128]{1,2,0:T(8,128)(2,1)}, bf16[1,256,128]{1,2,0:T(8,128)(2,1)S(1)}, u32[]{:S(2)}) copy-start(bf16[1,256,128]{1,2,0:T(8,128)(2,1)S(1)} %collective-permute-done) | copy-start | bytes 196612
  208.4 7.4 %collective-permute-start.1 = (bf16[1,256,128]{1,2,0:T(8,128)(2,1)S(1)}, bf16[1,256,128]{1,2,0:T(8,128)(2,1)S(1)}, u32[]{:S(2)}, u32[]{:S(2)}) collective-permute-start(bf16[1,256,128]{1,2,0:T(8,128)(2,1)S(1)} %collective-permute-done), channel_id=1, source_target_pairs={{0,8},{8,16},{16,24},{24,32},{32,40},{40,48},{48,56},{56,64},{64,7... | collective-permute-start | bytes 196616 | tf_op jit(solution)/shard_map/ppermute | solution.py:35
  211.9 12.7 %collective-permute-start.6 = (bf16[1,256,128]{1,2,0:T(8,128)(2,1)}, bf16[1,256,128]{1,2,0:T(8,128)(2,1)}, u32[]{:S(2)}, u32[]{:S(2)}) collective-permute-start(bf16[1,256,128]{1,2,0:T(8,128)(2,1)} %collective-permute-done.5), channel_id=1, source_target_pairs={{0,8},{8,16},{16,24},{24,32},{32,40},{40,48},{48,56},{56,64},{64,7... | collective-permute-start | bytes 196616 | tf_op jit(solution)/shard_map/ppermute | solution.py:35
  215.8 7.2 %copy-start.17 = (bf16[1,256,128]{1,2,0:T(8,128)(2,1)}, bf16[1,256,128]{1,2,0:T(8,128)(2,1)S(1)}, u32[]{:S(2)}) copy-start(bf16[1,256,128]{1,2,0:T(8,128)(2,1)S(1)} %collective-permute-done.1) | copy-start | bytes 196612
  216.5 11.6 %collective-permute-start.2 = (bf16[2,256,128]{1,2,0:T(8,128)(2,1)}, bf16[2,256,128]{1,2,0:T(8,128)(2,1)}, u32[]{:S(2)}, u32[]{:S(2)}) collective-permute-start(bf16[2,256,128]{1,2,0:T(8,128)(2,1)} %pad_maximum_fusion.9), channel_id=1, source_target_pairs={{0,16},{8,24},{16,32},{24,40},{32,48},{40,56},{48,64},{56,72},{64,... | collective-permute-start | bytes 393224 | tf_op jit(solution)/shard_map/ppermute | solution.py:35
  224.3 7.6 %copy-start.2 = (f32[256,4,128]{2,0,1:T(8,128)}, f32[256,4,128]{2,0,1:T(8,128)S(1)}, u32[]{:S(2)}) copy-start(f32[256,4,128]{2,0,1:T(8,128)S(1)} %maximum_multiply_fusion) | copy-start | bytes 1572868
  224.5 7.4 %copy-start.21 = (bf16[256,128]{0,1:T(8,128)(2,1)S(1)}, bf16[256,128]{0,1:T(8,128)(2,1)}, u32[]{:S(2)}) copy-start(bf16[256,128]{0,1:T(8,128)(2,1)} %copy-done.20) | copy-start | bytes 196612
  224.5 7.4 %copy-start.23 = (pred[256,256]{0,1:T(8,128)(4,1)S(1)}, pred[256,256]{0,1:T(8,128)(4,1)}, u32[]{:S(2)}) copy-start(pred[256,256]{0,1:T(8,128)(4,1)} %fusion.89) | copy-start | bytes 196612
  224.5 19.2 %copy-start.15 = (bf16[1,256,128]{1,2,0:T(8,128)(2,1)S(1)}, bf16[1,256,128]{1,2,0:T(8,128)(2,1)}, u32[]{:S(2)}) copy-start(bf16[1,256,128]{1,2,0:T(8,128)(2,1)} %copy-done.14) | copy-start | bytes 196612
  224.5 19.2 %copy-start.18 = (bf16[1,256,128]{1,2,0:T(8,128)(2,1)S(1)}, bf16[1,256,128]{1,2,0:T(8,128)(2,1)}, u32[]{:S(2)}) copy-start(bf16[1,256,128]{1,2,0:T(8,128)(2,1)} %copy-done.17) | copy-start | bytes 196612
  225.5 6.8 collective-permute-start.7
  229.2 13.8 %collective-permute-start.3 = (bf16[4,256,128]{1,2,0:T(8,128)(2,1)S(1)}, bf16[4,256,128]{1,2,0:T(8,128)(2,1)S(1)}, u32[]{:S(2)}, u32[]{:S(2)}) collective-permute-start(bf16[4,256,128]{1,2,0:T(8,128)(2,1)S(1)} %pad_maximum_fusion.3), channel_id=1, source_target_pairs={{0,32},{8,40},{16,48},{24,56},{32,64},{40,72},{48,80},{56,88},{64,... | collective-permute-start | bytes 786440 | tf_op jit(solution)/shard_map/ppermute | solution.py:35
  232.3 0.6 copy-start.9
  234.5 30.2 %collective-permute-start.8 = (bf16[4,256,128]{1,2,0:T(8,128)(2,1)}, bf16[4,256,128]{1,2,0:T(8,128)(2,1)}, u32[]{:S(2)}, u32[]{:S(2)}) collective-permute-start(bf16[4,256,128]{1,2,0:T(8,128)(2,1)} %pad_maximum_fusion.4), channel_id=1, source_target_pairs={{0,32},{8,40},{16,48},{24,56},{32,64},{40,72},{48,80},{56,88},{64,... | collective-permute-start | bytes 786440 | tf_op jit(solution)/shard_map/ppermute | solution.py:35
  243.0 0.7 copy-start.12
  245.4 32.9 %collective-permute-start.4 = (bf16[8,256,128]{1,2,0:T(8,128)(2,1)}, bf16[8,256,128]{1,2,0:T(8,128)(2,1)}, u32[]{:S(2)}, u32[]{:S(2)}) collective-permute-start(bf16[8,256,128]{1,2,0:T(8,128)(2,1)} %pad_maximum_fusion), channel_id=1, source_target_pairs={{0,64},{8,72},{16,80},{24,88},{32,96},{40,104},{48,112},{56,120},{... | collective-permute-start | bytes 1572872 | tf_op jit(solution)/shard_map/ppermute | solution.py:35
  263.0 1.7 copy-start.10
  263.0 17.2 %copy-start.13 = (bf16[4,256,128]{1,2,0:T(8,128)(2,1)S(1)}, bf16[4,256,128]{1,2,0:T(8,128)(2,1)}, u32[]{:S(2)}) copy-start(bf16[4,256,128]{1,2,0:T(8,128)(2,1)} %copy-done.12) | copy-start | bytes 786436
  263.1 19.4 %copy-start.19 = (bf16[1,256,128]{1,2,0:T(8,128)(2,1)S(1)}, bf16[1,256,128]{1,2,0:T(8,128)(2,1)}, u32[]{:S(2)}) copy-start(bf16[1,256,128]{1,2,0:T(8,128)(2,1)} %copy-done.17) | copy-start | bytes 196612
  263.1 20.1 %copy-start.16 = (bf16[1,256,128]{1,2,0:T(8,128)(2,1)S(1)}, bf16[1,256,128]{1,2,0:T(8,128)(2,1)}, u32[]{:S(2)}) copy-start(bf16[1,256,128]{1,2,0:T(8,128)(2,1)} %copy-done.14) | copy-start | bytes 196612
  266.7 32.6 %collective-permute-start.9 = (bf16[8,256,128]{1,2,0:T(8,128)(2,1)}, bf16[8,256,128]{1,2,0:T(8,128)(2,1)}, u32[]{:S(2)}, u32[]{:S(2)}) collective-permute-start(bf16[8,256,128]{1,2,0:T(8,128)(2,1)} %pad_maximum_fusion.1), channel_id=1, source_target_pairs={{0,64},{8,72},{16,80},{24,88},{32,96},{40,104},{48,112},{56,120},{... | collective-permute-start | bytes 1572872 | tf_op jit(solution)/shard_map/ppermute | solution.py:35
  380.6 0.9 copy-start.4
  452.4 23.5 %collective-permute-start.10 = (bf16[8,256,128]{1,2,0:T(8,128)(2,1)}, bf16[8,256,128]{1,2,0:T(8,128)(2,1)}, u32[]{:S(2)}, u32[]{:S(2)}) collective-permute-start(bf16[8,256,128]{1,2,0:T(8,128)(2,1)} %slice.232), channel_id=1, source_target_pairs={{64,0},{72,8},{80,16},{88,24},{96,32},{104,40},{112,48},{120,56},{... | collective-permute-start | bytes 1572872 | tf_op jit(solution)/shard_map/ppermute | solution.py:35
  453.6 7.5 %copy-start.3 = (f32[256,4,128]{2,0,1:T(8,128)S(1)}, f32[256,4,128]{2,0,1:T(8,128)}, u32[]{:S(2)}) copy-start(f32[256,4,128]{2,0,1:T(8,128)} %copy-done.2) | copy-start | bytes 1572868
  453.7 7.5 %copy-start.7 = (f32[256,128]{1,0:T(8,128)S(1)}, f32[256,128]{1,0:T(8,128)}, u32[]{:S(2)}) copy-start(f32[256,128]{1,0:T(8,128)} %copy.132) | copy-start | bytes 393220
  459.8 5.1 copy-start.8
  459.8 22.8 %collective-permute-start.15 = (bf16[8,256,128]{1,2,0:T(8,128)(2,1)}, bf16[8,256,128]{1,2,0:T(8,128)(2,1)}, u32[]{:S(2)}, u32[]{:S(2)}) collective-permute-start(bf16[8,256,128]{1,2,0:T(8,128)(2,1)} %slice.231), channel_id=1, source_target_pairs={{64,0},{72,8},{80,16},{88,24},{96,32},{104,40},{112,48},{120,56},{... | collective-permute-start | bytes 1572872 | tf_op jit(solution)/shard_map/ppermute | solution.py:35
  465.9 5.2 copy-start.22
  471.1 11.5 %copy-start.5 = (f32[8,256,128]{1,2,0:T(8,128)S(1)}, f32[8,256,128]{1,2,0:T(8,128)}, u32[]{:S(2)}) copy-start(f32[8,256,128]{1,2,0:T(8,128)} %copy.167) | copy-start | bytes 3145732
  477.4 7.7 %copy-start.6 = (bf16[256,4,128]{0,2,1:T(8,128)(2,1)S(1)}, bf16[256,4,128]{0,2,1:T(8,128)(2,1)}, u32[]{:S(2)}) copy-start(bf16[256,4,128]{0,2,1:T(8,128)(2,1)} %copy.165) | copy-start | bytes 786436
  477.5 34.4 %collective-permute-start.11 = (bf16[4,256,128]{1,2,0:T(8,128)(2,1)S(1)}, bf16[4,256,128]{1,2,0:T(8,128)(2,1)S(1)}, u32[]{:S(2)}, u32[]{:S(2)}) collective-permute-start(bf16[4,256,128]{1,2,0:T(8,128)(2,1)S(1)} %slice.234), channel_id=1, source_target_pairs={{32,0},{40,8},{48,16},{56,24},{64,32},{72,40},{80,48},{88,56},{96,... | collective-permute-start | bytes 786440 | tf_op jit(solution)/shard_map/ppermute | solution.py:35
  483.8 38.5 %collective-permute-start.16 = (bf16[4,256,128]{1,2,0:T(8,128)(2,1)S(1)}, bf16[4,256,128]{1,2,0:T(8,128)(2,1)S(1)}, u32[]{:S(2)}, u32[]{:S(2)}) collective-permute-start(bf16[4,256,128]{1,2,0:T(8,128)(2,1)S(1)} %slice.233), channel_id=1, source_target_pairs={{32,0},{40,8},{48,16},{56,24},{64,32},{72,40},{80,48},{88,56},{96,... | collective-permute-start | bytes 786440 | tf_op jit(solution)/shard_map/ppermute | solution.py:35
  512.0 22.6 %copy-start.25 = (f32[256,1,64]{0,2,1:T(8,128)S(1)}, f32[256,1,64]{0,2,1:T(8,128)}, u32[]{:S(2)}) copy-start(f32[256,1,64]{0,2,1:T(8,128)} %get-tuple-element.466) | copy-start | bytes 196612
  512.0 11.8 %collective-permute-start.12 = (bf16[2,256,128]{1,2,0:T(8,128)(2,1)S(1)}, bf16[2,256,128]{1,2,0:T(8,128)(2,1)S(1)}, u32[]{:S(2)}, u32[]{:S(2)}) collective-permute-start(bf16[2,256,128]{1,2,0:T(8,128)(2,1)S(1)} %slice.236), channel_id=1, source_target_pairs={{16,0},{24,8},{32,16},{40,24},{48,32},{56,40},{64,48},{72,56},{80,... | collective-permute-start | bytes 393224 | tf_op jit(solution)/shard_map/ppermute | solution.py:35
  522.3 14.9 %copy-start.1 = (bf16[8,256,512]{1,2,0:T(8,128)(2,1)S(1)}, bf16[8,256,512]{1,2,0:T(8,128)(2,1)}, u32[]{:S(2)}) copy-start(bf16[8,256,512]{1,2,0:T(8,128)(2,1)} %copy-done) | copy-start | bytes 6291460
  522.4 7.0 collective-permute-start.17
  523.9 6.8 collective-permute-start.13
  529.4 3.1 collective-permute-start.18
  530.7 3.8 collective-permute-start.14
  532.6 4.6 collective-permute-start.19
Sparse Core Ops, SparseCore 0:
  550.4 151.0 reduce-scatter.3
